TPU v7x, 256 devices: a whole 4x4x8 slice. The times are simulated.
256 devices in a mesh: gx: 64 (over z, y_lo, x), gy: 4 (over y_hi, core).
Axes of the slice: x: 4, y: 4 (y_hi: 2, y_lo: 2; y = y_hi * 2 + y_lo), z: 8, core: 2. Of those that a mesh axis runs over, the one named last changes fastest.
Arguments:
- misfit: float32 [3, 512, 128, 128], P(None, 'gx', 'gy'), may hold values from -13 to 13
- damage: float32 [512, 128, 128], P('gx', 'gy'), may hold values from 0 to 0.9
- displacement: float32 [3, 512, 128, 128], P(None, 'gx', 'gy'), may hold values from -3 to 3
Outputs:
- adjoint: float32 [3, 512, 128, 128], P(None, 'gx', 'gy')
- sensitivity: float32 [512, 128, 128], P('gx', 'gy')
All inputs are finite; a program needn't handle non-finite values.
Results may differ from a plain program's by a relative error of at most 0.00012.
Values sent between devices are 32-bit elements; how exact they have to be, the bound alone decides.
No kernel may reach another device: no remote copies, remote signals or barrier semaphores. Data moves between devices by JAX's collectives and lax.ppermute only.
A program may use at most 64 MiB of HBM per device.

v0:
```python
import math
import jax
import jax.numpy as jnp
import numpy as np
from jax import lax
from jax.sharding import Mesh
from jax.sharding import PartitionSpec as P

ITERS = 3
GX = ("gx_0", "gx_1", "gx_2")
GY = ("gy_0", "gy_1")
GX_GY = ("gx_0", "gx_1", "gx_2", "gy_0", "gy_1")


def passed_along(x, axis, by):
    devices = lax.axis_size(axis)
    pairs = [(i, i + by) for i in range(devices) if 0 <= i + by < devices]
    return lax.ppermute(x, axis, pairs)


def over_axes(x, axes):
    for axis in axes:
        x = lax.psum(x, axis)
    return x


def kronecker(first, second):
    return 1.0 if first == second else 0.0


def element_matrix():
    modulus = 3.0
    poisson_ratio = 0.3
    lame_first = modulus * poisson_ratio / ((1.0 + poisson_ratio) * (1.0 - 2.0 * poisson_ratio))
    shear_modulus = modulus / (2.0 * (1.0 + poisson_ratio))
    signs = [
        [
            2.0 * (corner_index >> 2 & 1) - 1.0,
            2.0 * (corner_index >> 1 & 1) - 1.0,
            2.0 * (corner_index & 1) - 1.0,
        ]
        for corner_index in range(8)
    ]
    elastic = [
        [
            [
                [
                    lame_first * kronecker(i, j) * kronecker(k, l)
                    + shear_modulus
                    * (kronecker(i, k) * kronecker(j, l) + kronecker(i, l) * kronecker(j, k))
                    for l in range(3)
                ]
                for k in range(3)
            ]
            for j in range(3)
        ]
        for i in range(3)
    ]
    stiffness = np.zeros((8, 3, 8, 3))
    root_three = math.sqrt(3.0)
    for gauss_index in range(8):
        gauss_point = [signs[gauss_index][dimension] / root_three for dimension in range(3)]
        gradients = [[0.0, 0.0, 0.0] for corner_index in range(8)]
        for corner_index in range(8):
            for dimension in range(3):
                factor = 0.25 * signs[corner_index][dimension]
                for others in range(3):
                    if others != dimension:
                        factor = factor * (1.0 + signs[corner_index][others] * gauss_point[others])
                gradients[corner_index][dimension] = factor
        for first_corner in range(8):
            for i in range(3):
                for second_corner in range(8):
                    for j in range(3):
                        accumulated = 0.0
                        for k in range(3):
                            for l in range(3):
                                accumulated = (
                                    accumulated
                                    + gradients[first_corner][k]
                                    * elastic[i][k][j][l]
                                    * gradients[second_corner][l]
                                )
                        stiffness[first_corner, i, second_corner, j] = (
                            stiffness[first_corner, i, second_corner, j] + 0.125 * accumulated
                        )
    return stiffness.reshape(24, 24)


def corner_offsets():
    return [
        (corner_index >> 2 & 1, corner_index >> 1 & 1, corner_index & 1)
        for corner_index in range(8)
    ]


def corner_stack(padded, count_x, count_y, count_z):
    return jnp.stack(
        [
            padded[
                :,
                shift_x : shift_x + count_x,
                shift_y : shift_y + count_y,
                shift_z : shift_z + count_z,
            ]
            for shift_x, shift_y, shift_z in corner_offsets()
        ],
        0,
    )


def element_forces(padded, degradation):
    count_x, count_y, count_z = degradation.shape
    stacked = corner_stack(padded, count_x, count_y, count_z).reshape(24, -1)
    table = jnp.asarray(element_matrix(), jnp.float32)
    forces = jnp.dot(
        table, stacked, precision=lax.Precision.HIGHEST, preferred_element_type=jnp.float32
    )
    return forces.reshape(8, 3, count_x, count_y, count_z) * degradation


def assemble(forces):
    total = None
    for corner_index, (shift_x, shift_y, shift_z) in enumerate(corner_offsets()):
        placed = jnp.pad(
            forces[corner_index],
            ((0, 0), (shift_x, 1 - shift_x), (shift_y, 1 - shift_y), (shift_z, 1 - shift_z)),
        )
        total = placed if total is None else total + placed
    return total


def apply_owned(field, degradation):
    rim_x = passed_along(field[:, :1], GX, -1)
    extended = jnp.concatenate([field, rim_x], 1)
    rim_y = passed_along(extended[:, :, :1], GY, -1)
    extended = jnp.concatenate([extended, rim_y], 2)
    extended = jnp.pad(extended, ((0, 0), (0, 0), (0, 0), (0, 1)))
    nodes = assemble(element_forces(extended, degradation))[:, :, :, :-1]
    spill_y = passed_along(nodes[:, :, -1:], GY, 1)
    nodes = jnp.concatenate([nodes[:, :, :1] + spill_y, nodes[:, :, 1:-1]], 2)
    spill_x = passed_along(nodes[:, -1:], GX, 1)
    return jnp.concatenate([nodes[:, :1] + spill_x, nodes[:, 1:-1]], 1)


def two_products(residual, image):
    return (
        over_axes(jnp.sum(residual * residual), GX_GY),
        over_axes(jnp.sum(residual * image), GX_GY),
    )


def body(misfit, damage, displacement):
    degradation = (1.0 - damage) * (1.0 - damage) + 0.001

    def operate(field):
        return apply_owned(field, degradation)

    adjoint = jnp.zeros_like(misfit)
    residual = misfit
    image = operate(residual)
    norm_now, product = two_products(residual, image)
    alpha = norm_now / product
    direction = residual
    along = image
    for step in range(ITERS):
        adjoint = adjoint + alpha * direction
        residual = residual - alpha * along
        if step + 1 < ITERS:
            image = operate(residual)
            norm_next, product = two_products(residual, image)
            ratio = norm_next / norm_now
            alpha = norm_next / (product - ratio * norm_next / alpha)
            direction = residual + ratio * direction
            along = image + ratio * along
            norm_now = norm_next
    count_x, count_y, count_z = damage.shape
    paired = jnp.concatenate([adjoint, displacement], 0)
    pair_x = passed_along(paired[:, :1], GX, -1)
    paired = jnp.concatenate([paired, pair_x], 1)
    pair_y = passed_along(paired[:, :, :1], GY, -1)
    paired = jnp.concatenate([paired, pair_y], 2)
    paired = jnp.pad(paired, ((0, 0), (0, 0), (0, 0), (0, 1)))
    table = jnp.asarray(element_matrix(), jnp.float32)
    adjoint_corners = corner_stack(paired[:3], count_x, count_y, count_z).reshape(24, -1)
    moved_corners = corner_stack(paired[3:], count_x, count_y, count_z).reshape(24, -1)
    product_terms = jnp.dot(
        table, moved_corners, precision=lax.Precision.HIGHEST, preferred_element_type=jnp.float32
    )
    contraction = jnp.sum(adjoint_corners * product_terms, 0).reshape(count_x, count_y, count_z)
    sensitivity = 2.0 * (1.0 - damage) * contraction
    return (adjoint, sensitivity)


def solution(mesh):
    split = Mesh(mesh.devices.reshape(8, 2, 4, 2, 2), ("gx_0", "gx_1", "gx_2", "gy_0", "gy_1"))
    in_specs = (P(None, GX, GY, None), P(GX, GY, None), P(None, GX, GY, None))
    out_specs = (P(None, GX, GY, None), P(GX, GY, None))
    return jax.shard_map(body, mesh=split, in_specs=in_specs, out_specs=out_specs, check_vma=False)
```

profile of v0, /device:TPU:7, one launch (start us, length us, event | category | flops | bytes accessed | tf_op | source)
XLA Modules:
  0.0 310.1 jit_solution(6029709115871913308)
XLA Ops:
  1.4 2.4 collective-permute-start
  8.4 3.7 %collective-permute-start.1 = (f32[3,9,1,128]{3,2,1,0:T(1,128)S(1)}, f32[3,9,1,128]{3,2,1,0:T(1,128)S(1)}, u32[]{:S(2)}, u32[]{:S(2)}) collective-permute-start(f32[3,9,1,128]{3,2,1,0:T(1,128)S(1)} %slice.407), channel_id=1, source_target_pairs={{1,0},{2,1},{3,2},{5,4},{6,5},{7,6},{9,8},{10,9},{11,10},{13,12},{... | collective-permute-start | bytes 41480 | tf_op jit(solution)/shard_map/ppermute | solution.py:18
  13.1 3.3 %collective-permute-done.1 = f32[3,9,1,128]{3,2,1,0:T(1,128)S(1)} collective-permute-done((f32[3,9,1,128]{3,2,1,0:T(1,128)S(1)}, f32[3,9,1,128]{3,2,1,0:T(1,128)S(1)}, u32[]{:S(2)}, u32[]{:S(2)}) %collective-permute-start.1) | collective-permute-done | bytes 13856 | tf_op jit(solution)/shard_map/ppermute | solution.py:18
  22.4 2.9 reshape.32
  25.4 2.8 convolution_bitcast_fusion.2
  30.6 1.9 collective-permute-start.2
  33.8 1.9 collective-permute-start.3
  35.7 2.9 collective-permute-done.3
  39.4 16.9 %all-reduce.30 = (f32[]{:T(128)}, f32[]{:T(128)}) all-reduce(f32[]{:T(128)} %get-tuple-element.7, f32[]{:T(128)} %get-tuple-element.6), channel_id=1, replica_groups=mesh['gx_0'=8,'gx_1'=2,'gx_2'=4,'gy_0'=2,'gy_1'=2] {'gx_0'}, use_global_device_ids=true, to_apply=%region_1.2 | all-reduce | flops 2 | bytes 16 | tf_op jit(solution)/shard_map/psum | solution.py:23
  56.3 4.6 %all-reduce.42 = (f32[]{:T(128)}, f32[]{:T(128)}) all-reduce(f32[]{:T(128)} %get-tuple-element.12, f32[]{:T(128)} %get-tuple-element.13), channel_id=1, replica_groups=mesh['gx_0'=8,'gx_1'=2,'gx_2'=4,'gy_0'=2,'gy_1'=2] {'gx_1'}, use_global_device_ids=true, to_apply=%region_2.3 | all-reduce | flops 2 | bytes 16 | tf_op jit(solution)/shard_map/psum | solution.py:23
  60.9 9.1 %all-reduce.33 = (f32[]{:T(128)}, f32[]{:T(128)}) all-reduce(f32[]{:T(128)} %get-tuple-element.36, f32[]{:T(128)} %get-tuple-element.37), channel_id=1, replica_groups=mesh['gx_0'=8,'gx_1'=2,'gx_2'=4,'gy_0'=2,'gy_1'=2] {'gx_2'}, use_global_device_ids=true, to_apply=%region_3.4 | all-reduce | flops 2 | bytes 16 | tf_op jit(solution)/shard_map/psum | solution.py:23
  70.0 5.9 %all-reduce.39 = (f32[]{:T(128)}, f32[]{:T(128)}) all-reduce(f32[]{:T(128)} %get-tuple-element.18, f32[]{:T(128)} %get-tuple-element.19), channel_id=1, replica_groups=mesh['gx_0'=8,'gx_1'=2,'gx_2'=4,'gy_0'=2,'gy_1'=2] {'gy_0'}, use_global_device_ids=true, to_apply=%region_4.5 | all-reduce | flops 2 | bytes 16 | tf_op jit(solution)/shard_map/psum | solution.py:23
  75.9 12.1 %all-reduce.36 = (f32[]{:T(128)}, f32[]{:T(128)}) all-reduce(f32[]{:T(128)} %get-tuple-element.30, f32[]{:T(128)} %get-tuple-element.31), channel_id=1, replica_groups=mesh['gx_0'=8,'gx_1'=2,'gx_2'=4,'gy_0'=2,'gy_1'=2] {'gy_1'}, use_global_device_ids=true, to_apply=%region_5.6 | all-reduce | flops 2 | bytes 16 | tf_op jit(solution)/shard_map/psum | solution.py:23
  90.2 1.9 collective-permute-start.4
  92.1 5.0 %collective-permute-done.4 = f32[3,1,32,128]{3,2,1,0:T(8,128)S(1)} collective-permute-done((f32[3,1,32,128]{3,2,1,0:T(8,128)S(1)}, f32[3,1,32,128]{3,2,1,0:T(8,128)S(1)}, u32[]{:S(2)}, u32[]{:S(2)}) %collective-permute-start.4) | collective-permute-done | bytes 49184 | tf_op jit(solution)/shard_map/ppermute | solution.py:18
  97.2 3.6 %collective-permute-start.5 = (f32[3,9,1,128]{3,2,1,0:T(1,128)S(1)}, f32[3,9,1,128]{3,2,1,0:T(1,128)S(1)}, u32[]{:S(2)}, u32[]{:S(2)}) collective-permute-start(f32[3,9,1,128]{3,2,1,0:T(1,128)S(1)} %pad_maximum_fusion.14), channel_id=1, source_target_pairs={{1,0},{2,1},{3,2},{5,4},{6,5},{7,6},{9,8},{10,9},{11,10},{13,12},{... | collective-permute-start | bytes 41480 | tf_op jit(solution)/shard_map/ppermute | solution.py:18
  100.8 4.3 %collective-permute-done.5 = f32[3,9,1,128]{3,2,1,0:T(1,128)S(1)} collective-permute-done((f32[3,9,1,128]{3,2,1,0:T(1,128)S(1)}, f32[3,9,1,128]{3,2,1,0:T(1,128)S(1)}, u32[]{:S(2)}, u32[]{:S(2)}) %collective-permute-start.5) | collective-permute-done | bytes 13856 | tf_op jit(solution)/shard_map/ppermute | solution.py:18
  111.2 4.6 %reshape.34 = f32[24,32768]{1,0:T(8,128)} reshape(f32[8,3,8,32,128]{4,3,2,1,0:T(8,128)} %fusion.22) | data formatting | bytes 6291456 | tf_op jit(solution)/shard_map/reshape | solution.py:114
  115.9 4.7 %convolution_bitcast_fusion.1 = f32[3,8,256,128]{3,1,2,0:T(8,128)S(1)} fusion(f32[24,24]{1,0:T(8,128)S(1)} %copy-done.5, f32[24,32768]{1,0:T(8,128)} %reshape.34), kind=kOutput, calls=%fused_computation.10 | convolution fusion | flops 226492416 | bytes 6293760 | tf_op jit(solution)/shard_map/dot_general | solution.py:116
  123.0 1.9 collective-permute-start.6
  126.1 1.9 collective-permute-start.7
  128.0 2.9 collective-permute-done.7
  131.8 11.4 %all-reduce.29 = (f32[]{:T(128)}, f32[]{:T(128)}) all-reduce(f32[]{:T(128)} %get-tuple-element.5, f32[]{:T(128)} %get-tuple-element.4), channel_id=1, replica_groups=mesh['gx_0'=8,'gx_1'=2,'gx_2'=4,'gy_0'=2,'gy_1'=2] {'gx_0'}, use_global_device_ids=true, to_apply=%region_13.14 | all-reduce | flops 2 | bytes 16 | tf_op jit(solution)/shard_map/psum | solution.py:23
  143.2 4.5 %all-reduce.41 = (f32[]{:T(128)}, f32[]{:T(128)}) all-reduce(f32[]{:T(128)} %get-tuple-element.10, f32[]{:T(128)} %get-tuple-element.11), channel_id=1, replica_groups=mesh['gx_0'=8,'gx_1'=2,'gx_2'=4,'gy_0'=2,'gy_1'=2] {'gx_1'}, use_global_device_ids=true, to_apply=%region_14.15 | all-reduce | flops 2 | bytes 16 | tf_op jit(solution)/shard_map/psum | solution.py:23
  147.6 7.9 %all-reduce.32 = (f32[]{:T(128)}, f32[]{:T(128)}) all-reduce(f32[]{:T(128)} %get-tuple-element.34, f32[]{:T(128)} %get-tuple-element.35), channel_id=1, replica_groups=mesh['gx_0'=8,'gx_1'=2,'gx_2'=4,'gy_0'=2,'gy_1'=2] {'gx_2'}, use_global_device_ids=true, to_apply=%region_15.16 | all-reduce | flops 2 | bytes 16 | tf_op jit(solution)/shard_map/psum | solution.py:23
  155.5 6.0 %all-reduce.38 = (f32[]{:T(128)}, f32[]{:T(128)}) all-reduce(f32[]{:T(128)} %get-tuple-element.16, f32[]{:T(128)} %get-tuple-element.17), channel_id=1, replica_groups=mesh['gx_0'=8,'gx_1'=2,'gx_2'=4,'gy_0'=2,'gy_1'=2] {'gy_0'}, use_global_device_ids=true, to_apply=%region_16.17 | all-reduce | flops 2 | bytes 16 | tf_op jit(solution)/shard_map/psum | solution.py:23
  161.5 12.4 %all-reduce.35 = (f32[]{:T(128)}, f32[]{:T(128)}) all-reduce(f32[]{:T(128)} %get-tuple-element.28, f32[]{:T(128)} %get-tuple-element.29), channel_id=1, replica_groups=mesh['gx_0'=8,'gx_1'=2,'gx_2'=4,'gy_0'=2,'gy_1'=2] {'gy_1'}, use_global_device_ids=true, to_apply=%region_17.18 | all-reduce | flops 2 | bytes 16 | tf_op jit(solution)/shard_map/psum | solution.py:23
  179.2 1.9 collective-permute-start.8
  181.1 5.0 %collective-permute-done.8 = f32[3,1,32,128]{3,2,1,0:T(8,128)S(1)} collective-permute-done((f32[3,1,32,128]{3,2,1,0:T(8,128)S(1)}, f32[3,1,32,128]{3,2,1,0:T(8,128)S(1)}, u32[]{:S(2)}, u32[]{:S(2)}) %collective-permute-start.8) | collective-permute-done | bytes 49184 | tf_op jit(solution)/shard_map/ppermute | solution.py:18
  186.2 3.6 %collective-permute-start.9 = (f32[3,9,1,128]{3,2,1,0:T(1,128)S(1)}, f32[3,9,1,128]{3,2,1,0:T(1,128)S(1)}, u32[]{:S(2)}, u32[]{:S(2)}) collective-permute-start(f32[3,9,1,128]{3,2,1,0:T(1,128)S(1)} %pad_maximum_fusion.13), channel_id=1, source_target_pairs={{1,0},{2,1},{3,2},{5,4},{6,5},{7,6},{9,8},{10,9},{11,10},{13,12},{... | collective-permute-start | bytes 41480 | tf_op jit(solution)/shard_map/ppermute | solution.py:18
  189.8 4.3 %collective-permute-done.9 = f32[3,9,1,128]{3,2,1,0:T(1,128)S(1)} collective-permute-done((f32[3,9,1,128]{3,2,1,0:T(1,128)S(1)}, f32[3,9,1,128]{3,2,1,0:T(1,128)S(1)}, u32[]{:S(2)}, u32[]{:S(2)}) %collective-permute-start.9) | collective-permute-done | bytes 13856 | tf_op jit(solution)/shard_map/ppermute | solution.py:18
  200.2 4.6 %reshape.36 = f32[24,32768]{1,0:T(8,128)} reshape(f32[8,3,8,32,128]{4,3,2,1,0:T(8,128)} %fusion.30) | data formatting | bytes 6291456 | tf_op jit(solution)/shard_map/reshape | solution.py:114
  204.9 4.7 %convolution_bitcast_fusion = f32[3,8,256,128]{3,1,2,0:T(8,128)S(1)} fusion(f32[24,24]{1,0:T(8,128)S(1)} %copy-done.5, f32[24,32768]{1,0:T(8,128)} %reshape.36), kind=kOutput, calls=%fused_computation.9 | convolution fusion | flops 226492416 | bytes 6293760 | tf_op jit(solution)/shard_map/dot_general | solution.py:116
  212.1 2.1 collective-permute-start.10
  215.3 1.9 collective-permute-start.11
  217.2 2.9 collective-permute-done.11
  220.9 12.4 %all-reduce.28 = (f32[]{:T(128)}, f32[]{:T(128)}) all-reduce(f32[]{:T(128)} %get-tuple-element.3, f32[]{:T(128)} %get-tuple-element.2), channel_id=1, replica_groups=mesh['gx_0'=8,'gx_1'=2,'gx_2'=4,'gy_0'=2,'gy_1'=2] {'gx_0'}, use_global_device_ids=true, to_apply=%region_25.26 | all-reduce | flops 2 | bytes 16 | tf_op jit(solution)/shard_map/psum | solution.py:23
  233.3 4.6 %all-reduce.40 = (f32[]{:T(128)}, f32[]{:T(128)}) all-reduce(f32[]{:T(128)} %get-tuple-element.8, f32[]{:T(128)} %get-tuple-element.9), channel_id=1, replica_groups=mesh['gx_0'=8,'gx_1'=2,'gx_2'=4,'gy_0'=2,'gy_1'=2] {'gx_1'}, use_global_device_ids=true, to_apply=%region_26.27 | all-reduce | flops 2 | bytes 16 | tf_op jit(solution)/shard_map/psum | solution.py:23
  237.9 8.1 %all-reduce.31 = (f32[]{:T(128)}, f32[]{:T(128)}) all-reduce(f32[]{:T(128)} %get-tuple-element.32, f32[]{:T(128)} %get-tuple-element.33), channel_id=1, replica_groups=mesh['gx_0'=8,'gx_1'=2,'gx_2'=4,'gy_0'=2,'gy_1'=2] {'gx_2'}, use_global_device_ids=true, to_apply=%region_27.28 | all-reduce | flops 2 | bytes 16 | tf_op jit(solution)/shard_map/psum | solution.py:23
  246.0 5.9 %all-reduce.37 = (f32[]{:T(128)}, f32[]{:T(128)}) all-reduce(f32[]{:T(128)} %get-tuple-element.14, f32[]{:T(128)} %get-tuple-element.15), channel_id=1, replica_groups=mesh['gx_0'=8,'gx_1'=2,'gx_2'=4,'gy_0'=2,'gy_1'=2] {'gy_0'}, use_global_device_ids=true, to_apply=%region_28.29 | all-reduce | flops 2 | bytes 16 | tf_op jit(solution)/shard_map/psum | solution.py:23
  251.9 12.1 %all-reduce.34 = (f32[]{:T(128)}, f32[]{:T(128)}) all-reduce(f32[]{:T(128)} %get-tuple-element.26, f32[]{:T(128)} %get-tuple-element.27), channel_id=1, replica_groups=mesh['gx_0'=8,'gx_1'=2,'gx_2'=4,'gy_0'=2,'gy_1'=2] {'gy_1'}, use_global_device_ids=true, to_apply=%region_29.30 | all-reduce | flops 2 | bytes 16 | tf_op jit(solution)/shard_map/psum | solution.py:23
  268.7 1.9 collective-permute-start.12
  270.7 6.1 %collective-permute-done.12 = f32[6,1,32,128]{3,2,1,0:T(8,128)S(1)} collective-permute-done((f32[6,1,32,128]{3,2,1,0:T(8,128)S(1)}, f32[6,1,32,128]{3,2,1,0:T(8,128)S(1)}, u32[]{:S(2)}, u32[]{:S(2)}) %collective-permute-start.12) | collective-permute-done | bytes 98336 | tf_op jit(solution)/shard_map/ppermute | solution.py:18
  276.8 3.1 %collective-permute-start.13 = (f32[6,9,1,128]{3,2,1,0:T(1,128)S(1)}, f32[6,9,1,128]{3,2,1,0:T(1,128)S(1)}, u32[]{:S(2)}, u32[]{:S(2)}) collective-permute-start(f32[6,9,1,128]{3,2,1,0:T(1,128)S(1)} %pad_maximum_fusion.12), channel_id=1, source_target_pairs={{1,0},{2,1},{3,2},{5,4},{6,5},{7,6},{9,8},{10,9},{11,10},{13,12},{... | collective-permute-start | bytes 82952 | tf_op jit(solution)/shard_map/ppermute | solution.py:18
  280.7 3.9 %collective-permute-done.13 = f32[6,9,1,128]{3,2,1,0:T(1,128)S(1)} collective-permute-done((f32[6,9,1,128]{3,2,1,0:T(1,128)S(1)}, f32[6,9,1,128]{3,2,1,0:T(1,128)S(1)}, u32[]{:S(2)}, u32[]{:S(2)}) %collective-permute-start.13) | collective-permute-done | bytes 27680 | tf_op jit(solution)/shard_map/ppermute | solution.py:18
  291.5 4.6 %reshape.39 = f32[24,32768]{1,0:T(8,128)} reshape(f32[8,3,8,32,128]{4,3,2,1,0:T(8,128)} %get-tuple-element.68) | data formatting | bytes 6291456 | tf_op jit(solution)/shard_map/reshape | solution.py:186
  299.6 4.8 %reshape.38 = f32[24,32768]{1,0:T(8,128)} reshape(f32[8,3,8,32,128]{4,3,2,1,0:T(8,128)} %fusion.38) | data formatting | bytes 6291456 | tf_op jit(solution)/shard_map/reshape | solution.py:185
  304.4 5.0 %fusion = f32[32768]{0:T(1024)S(1)} fusion(f32[24,32768]{1,0:T(8,128)} %reshape.38, f32[24,24]{1,0:T(8,128)S(1)} %copy-done.5, f32[24,32768]{1,0:T(8,128)S(1)} %copy-done.2), kind=kOutput, calls=%fused_computation.27 | convolution fusion | flops 228032512 | bytes 6424832 | tf_op jit(solution)/shard_map/dot_general | solution.py:187
  (99 shorter events, 52.3 us)
Async XLA Ops:
  1.4 6.9 %collective-permute-start = (f32[3,1,32,128]{3,2,1,0:T(8,128)S(1)}, f32[3,1,32,128]{3,2,1,0:T(8,128)S(1)}, u32[]{:S(2)}, u32[]{:S(2)}) collective-permute-start(f32[3,1,32,128]{3,2,1,0:T(8,128)S(1)} %slice.322), channel_id=1, source_target_pairs={{4,0},{8,4},{12,8},{16,12},{20,16},{24,20},{28,24},{32,28},{36,32}... | collective-permute-start | bytes 147464 | tf_op jit(solution)/shard_map/ppermute | solution.py:18
  8.4 7.9 %collective-permute-start.1 = (f32[3,9,1,128]{3,2,1,0:T(1,128)S(1)}, f32[3,9,1,128]{3,2,1,0:T(1,128)S(1)}, u32[]{:S(2)}, u32[]{:S(2)}) collective-permute-start(f32[3,9,1,128]{3,2,1,0:T(1,128)S(1)} %slice.407), channel_id=1, source_target_pairs={{1,0},{2,1},{3,2},{5,4},{6,5},{7,6},{9,8},{10,9},{11,10},{13,12},{... | collective-permute-start | bytes 41480 | tf_op jit(solution)/shard_map/ppermute | solution.py:18
  22.4 2.9 copy-start.5
  29.6 9.0 %copy-start.3 = (f32[3,8,32,128]{3,2,1,0:T(8,128)S(1)}, f32[3,8,32,128]{3,2,1,0:T(8,128)}, u32[]{:S(2)}) copy-start(f32[3,8,32,128]{3,2,1,0:T(8,128)} %param.7) | copy-start | bytes 1179652
  30.6 3.1 collective-permute-start.2
  33.8 4.8 %collective-permute-start.3 = (f32[3,1,32,128]{3,2,1,0:T(8,128)S(1)}, f32[3,1,32,128]{3,2,1,0:T(8,128)S(1)}, u32[]{:S(2)}, u32[]{:S(2)}) collective-permute-start(f32[3,1,32,128]{3,2,1,0:T(8,128)S(1)} %pad_maximum_fusion.11), channel_id=1, source_target_pairs={{0,4},{4,8},{8,12},{12,16},{16,20},{20,24},{24,28},{28,32},{32,36}... | collective-permute-start | bytes 147464 | tf_op jit(solution)/shard_map/ppermute | solution.py:18
  90.2 6.9 %collective-permute-start.4 = (f32[3,1,32,128]{3,2,1,0:T(8,128)S(1)}, f32[3,1,32,128]{3,2,1,0:T(8,128)S(1)}, u32[]{:S(2)}, u32[]{:S(2)}) collective-permute-start(f32[3,1,32,128]{3,2,1,0:T(8,128)S(1)} %slice.424), channel_id=1, source_target_pairs={{4,0},{8,4},{12,8},{16,12},{20,16},{24,20},{28,24},{32,28},{36,32}... | collective-permute-start | bytes 147464 | tf_op jit(solution)/shard_map/ppermute | solution.py:18
  97.2 7.9 %collective-permute-start.5 = (f32[3,9,1,128]{3,2,1,0:T(1,128)S(1)}, f32[3,9,1,128]{3,2,1,0:T(1,128)S(1)}, u32[]{:S(2)}, u32[]{:S(2)}) collective-permute-start(f32[3,9,1,128]{3,2,1,0:T(1,128)S(1)} %pad_maximum_fusion.14), channel_id=1, source_target_pairs={{1,0},{2,1},{3,2},{5,4},{6,5},{7,6},{9,8},{10,9},{11,10},{13,12},{... | collective-permute-start | bytes 41480 | tf_op jit(solution)/shard_map/ppermute | solution.py:18
  123.0 3.1 collective-permute-start.6
  126.1 4.8 %collective-permute-start.7 = (f32[3,1,32,128]{3,2,1,0:T(8,128)S(1)}, f32[3,1,32,128]{3,2,1,0:T(8,128)S(1)}, u32[]{:S(2)}, u32[]{:S(2)}) collective-permute-start(f32[3,1,32,128]{3,2,1,0:T(8,128)S(1)} %pad_maximum_fusion.10), channel_id=1, source_target_pairs={{0,4},{4,8},{8,12},{12,16},{16,20},{20,24},{24,28},{28,32},{32,36}... | collective-permute-start | bytes 147464 | tf_op jit(solution)/shard_map/ppermute | solution.py:18
  179.2 6.9 %collective-permute-start.8 = (f32[3,1,32,128]{3,2,1,0:T(8,128)S(1)}, f32[3,1,32,128]{3,2,1,0:T(8,128)S(1)}, u32[]{:S(2)}, u32[]{:S(2)}) collective-permute-start(f32[3,1,32,128]{3,2,1,0:T(8,128)S(1)} %slice.438), channel_id=1, source_target_pairs={{4,0},{8,4},{12,8},{16,12},{20,16},{24,20},{28,24},{32,28},{36,32}... | collective-permute-start | bytes 147464 | tf_op jit(solution)/shard_map/ppermute | solution.py:18
  186.2 7.9 %collective-permute-start.9 = (f32[3,9,1,128]{3,2,1,0:T(1,128)S(1)}, f32[3,9,1,128]{3,2,1,0:T(1,128)S(1)}, u32[]{:S(2)}, u32[]{:S(2)}) collective-permute-start(f32[3,9,1,128]{3,2,1,0:T(1,128)S(1)} %pad_maximum_fusion.13), channel_id=1, source_target_pairs={{1,0},{2,1},{3,2},{5,4},{6,5},{7,6},{9,8},{10,9},{11,10},{13,12},{... | collective-permute-start | bytes 41480 | tf_op jit(solution)/shard_map/ppermute | solution.py:18
  212.0 56.7 %copy-start = (f32[3,8,32,128]{3,2,1,0:T(8,128)S(1)}, f32[3,8,32,128]{3,2,1,0:T(8,128)}, u32[]{:S(2)}) copy-start(f32[3,8,32,128]{3,2,1,0:T(8,128)} %param.9) | copy-start | bytes 1179652
  212.1 3.2 %collective-permute-start.10 = (f32[3,9,1,128]{3,2,1,0:T(1,128)S(1)}, f32[3,9,1,128]{3,2,1,0:T(1,128)S(1)}, u32[]{:S(2)}, u32[]{:S(2)}) collective-permute-start(f32[3,9,1,128]{3,2,1,0:T(1,128)S(1)} %slice.450), channel_id=1, source_target_pairs={{0,1},{1,2},{2,3},{4,5},{5,6},{6,7},{8,9},{9,10},{10,11},{12,13},{... | collective-permute-start | bytes 41480 | tf_op jit(solution)/shard_map/ppermute | solution.py:18
  215.3 4.8 %collective-permute-start.11 = (f32[3,1,32,128]{3,2,1,0:T(8,128)S(1)}, f32[3,1,32,128]{3,2,1,0:T(8,128)S(1)}, u32[]{:S(2)}, u32[]{:S(2)}) collective-permute-start(f32[3,1,32,128]{3,2,1,0:T(8,128)S(1)} %pad_maximum_fusion.9), channel_id=1, source_target_pairs={{0,4},{4,8},{8,12},{12,16},{16,20},{20,24},{24,28},{28,32},{32,36}... | collective-permute-start | bytes 147464 | tf_op jit(solution)/shard_map/ppermute | solution.py:18
  268.7 27.4 %copy-start.1 = (f32[3,8,32,128]{3,2,1,0:T(8,128)}, f32[3,8,32,128]{3,2,1,0:T(8,128)S(1)}, u32[]{:S(2)}) copy-start(f32[3,8,32,128]{3,2,1,0:T(8,128)S(1)} %get-tuple-element.39) | copy-start | bytes 1179652
  268.7 8.0 %collective-permute-start.12 = (f32[6,1,32,128]{3,2,1,0:T(8,128)S(1)}, f32[6,1,32,128]{3,2,1,0:T(8,128)S(1)}, u32[]{:S(2)}, u32[]{:S(2)}) collective-permute-start(f32[6,1,32,128]{3,2,1,0:T(8,128)S(1)} %pad_maximum_fusion.8), channel_id=1, source_target_pairs={{4,0},{8,4},{12,8},{16,12},{20,16},{24,20},{28,24},{32,28},{36,32}... | collective-permute-start | bytes 294920 | tf_op jit(solution)/shard_map/ppermute | solution.py:18
  276.8 7.8 %collective-permute-start.13 = (f32[6,9,1,128]{3,2,1,0:T(1,128)S(1)}, f32[6,9,1,128]{3,2,1,0:T(1,128)S(1)}, u32[]{:S(2)}, u32[]{:S(2)}) collective-permute-start(f32[6,9,1,128]{3,2,1,0:T(1,128)S(1)} %pad_maximum_fusion.12), channel_id=1, source_target_pairs={{1,0},{2,1},{3,2},{5,4},{6,5},{7,6},{9,8},{10,9},{11,10},{13,12},{... | collective-permute-start | bytes 82952 | tf_op jit(solution)/shard_map/ppermute | solution.py:18
  299.6 4.8 %copy-start.2 = (f32[24,32768]{1,0:T(8,128)S(1)}, f32[24,32768]{1,0:T(8,128)}, u32[]{:S(2)}) copy-start(f32[24,32768]{1,0:T(8,128)} %reshape.39) | copy-start | bytes 9437188
  304.4 5.0 %copy-start.4 = (f32[8,32,128]{2,1,0:T(8,128)S(1)}, f32[8,32,128]{2,1,0:T(8,128)}, u32[]{:S(2)}) copy-start(f32[8,32,128]{2,1,0:T(8,128)} %param.8) | copy-start | bytes 393220
where the time goes:
time: 312 us; the launch traced here: 310 us
  blocking collectives  134 us (43%)
  local copies, waits for them, and re-layouts  52.8 us (17%)
  waiting for transfers between devices  45.5 us (15%)
  starting transfers between devices  33.9 us (11%)
  matrix products  17.1 us (5%)
  other arithmetic  16.3 us (5%)
  between operations  10.7 us (3%)
    psum x15, blocking collectives, over_axes(): x = lax.psum(x, axis)  134 us
    ppermute x14, waiting for transfers between devices, passed_along(): return lax.ppermute(x, axis, pairs)  45.5 us
    ppermute x14, starting transfers between devices, passed_along(): return lax.ppermute(x, axis, pairs)  33.9 us
    unnamed x39, local copies, waits for them, and re-layouts  24.1 us
    reshape x3, local copies, waits for them, and re-layouts, element_forces(): stacked = corner_stack(padded, count_x, count_y, count_z).reshape(24, -1)  12.2 us
    dot_general x3, matrix products, element_forces(): jnp.dot(table, stacked, precision=lax.Precision.HIGHEST, preferred_elemen...  12.1 us
    unnamed x9, other arithmetic  7.31 us
  transfers between devices with their start and end apart: 14, of which 14 were waited for; matrix products, arithmetic and copies ran while one was open for 1% of the time, Pallas kernels for 0%

commit v1 on v0

--- a/solution.py
+++ b/solution.py
@@ -20,7 +20,7 @@
 
 def over_axes(x, axes):
     for axis in axes:
-        x = lax.psum(x, axis)
+        x = lax.all_gather(x, axis_name=axis).sum(axis=0)
     return x
 
 

time: 312 us -> 366 us (1.17)
  local copies, waits for them, and re-layouts: 52.8 us -> 97.6 us
  other arithmetic: 16.3 us -> 35.4 us
  blocking collectives: 134 us -> 124 us
    psum x15 -> x0, blocking collectives: 134 us -> none  [over_axes(): x = lax.psum(x, axis)]
    unnamed x0 -> x15, blocking collectives: none -> 124 us
    unnamed x39 -> x114, local copies, waits for them, and re-layouts: 24.1 us -> 69 us
    reduce_sum x0 -> x30, other arithmetic: none -> 19.1 us  [over_axes(): x = lax.all_gather(x, axis_name=axis).sum(axis=0)]
where the time goes in v1:
time: 366 us; the launch traced here: 364 us
  blocking collectives  124 us (34%)
  local copies, waits for them, and re-layouts  97.6 us (27%)
  waiting for transfers between devices  44.7 us (12%)
  other arithmetic  35.4 us (10%)
  starting transfers between devices  34.2 us (9%)
  matrix products  17.1 us (5%)
  between operations  11.2 us (3%)
    unnamed x15, blocking collectives  124 us
    unnamed x114, local copies, waits for them, and re-layouts  69 us
    ppermute x14, waiting for transfers between devices, passed_along(): return lax.ppermute(x, axis, pairs)  44.7 us
    ppermute x14, starting transfers between devices, passed_along(): return lax.ppermute(x, axis, pairs)  34.2 us
    reduce_sum x30, other arithmetic, over_axes(): x = lax.all_gather(x, axis_name=axis).sum(axis=0)  19.1 us
    reshape x3, local copies, waits for them, and re-layouts, element_forces(): stacked = corner_stack(padded, count_x, count_y, count_z).reshape(24, -1)  12.2 us
    dot_general x3, matrix products, element_forces(): jnp.dot(table, stacked, precision=lax.Precision.HIGHEST, preferred_elemen...  12.1 us
  transfers between devices with their start and end apart: 14, of which 14 were waited for; matrix products, arithmetic and copies ran while one was open for 1% of the time, Pallas kernels for 0%

profile of v1, /device:TPU:7, one launch (start us, length us, event | category | flops | bytes accessed | tf_op | source)
XLA Modules:
  0.0 364.0 jit_solution(4921738198780104436)
XLA Ops:
  1.4 2.4 collective-permute-start
  8.4 3.7 %collective-permute-start.1 = (f32[3,9,1,128]{3,2,1,0:T(1,128)S(1)}, f32[3,9,1,128]{3,2,1,0:T(1,128)S(1)}, u32[]{:S(2)}, u32[]{:S(2)}) collective-permute-start(f32[3,9,1,128]{3,2,1,0:T(1,128)S(1)} %slice.407), channel_id=1, source_target_pairs={{1,0},{2,1},{3,2},{5,4},{6,5},{7,6},{9,8},{10,9},{11,10},{13,12},{... | collective-permute-start | bytes 41480 | tf_op jit(solution)/shard_map/ppermute | solution.py:18
  13.1 3.3 collective-permute-done.1
  22.4 2.9 reshape.32
  25.4 2.8 convolution_bitcast_fusion.2
  30.8 1.9 collective-permute-start.2
  33.9 1.9 collective-permute-start.3
  36.4 2.3 collective-permute-done.3
  42.8 16.2 %all-reduce.60 = (f32[8]{0:T(128)S(1)}, f32[8]{0:T(128)S(1)}) all-reduce(f32[8]{0:T(128)S(1)} %dynamic-update-slice, f32[8]{0:T(128)S(1)} %dynamic-update-slice.5), channel_id=1, replica_groups=mesh['gx_0'=8,'gx_1'=2,'gx_2'=4,'gy_0'=2,'gy_1'=2] {'gx_0'}, use_global_device_ids=true, to_apply=%add.28 | all-reduce | flops 16 | bytes 128
  63.7 3.8 %all-reduce.72 = (f32[2]{0:T(128)S(1)}, f32[2]{0:T(128)S(1)}) all-reduce(f32[2]{0:T(128)S(1)} %dynamic-update-slice.1, f32[2]{0:T(128)S(1)} %dynamic-update-slice.6), channel_id=1, replica_groups=mesh['gx_0'=8,'gx_1'=2,'gx_2'=4,'gy_0'=2,'gy_1'=2] {'gx_1'}, use_global_device_ids=true, to_apply=%add.29 | all-reduce | flops 4 | bytes 32
  72.3 8.5 %all-reduce.63 = (f32[4]{0:T(128)S(1)}, f32[4]{0:T(128)S(1)}) all-reduce(f32[4]{0:T(128)S(1)} %dynamic-update-slice.2, f32[4]{0:T(128)S(1)} %dynamic-update-slice.7), channel_id=1, replica_groups=mesh['gx_0'=8,'gx_1'=2,'gx_2'=4,'gy_0'=2,'gy_1'=2] {'gx_2'}, use_global_device_ids=true, to_apply=%add.30 | all-reduce | flops 8 | bytes 64
  85.5 5.3 %all-reduce.69 = (f32[2]{0:T(128)S(1)}, f32[2]{0:T(128)S(1)}) all-reduce(f32[2]{0:T(128)S(1)} %dynamic-update-slice.3, f32[2]{0:T(128)S(1)} %dynamic-update-slice.8), channel_id=1, replica_groups=mesh['gx_0'=8,'gx_1'=2,'gx_2'=4,'gy_0'=2,'gy_1'=2] {'gy_0'}, use_global_device_ids=true, to_apply=%add.31 | all-reduce | flops 4 | bytes 32
  94.8 11.7 %all-reduce.66 = (f32[2]{0:T(128)S(1)}, f32[2]{0:T(128)S(1)}) all-reduce(f32[2]{0:T(128)S(1)} %dynamic-update-slice.4, f32[2]{0:T(128)S(1)} %dynamic-update-slice.9), channel_id=1, replica_groups=mesh['gx_0'=8,'gx_1'=2,'gx_2'=4,'gy_0'=2,'gy_1'=2] {'gy_1'}, use_global_device_ids=true, to_apply=%add.32 | all-reduce | flops 4 | bytes 32
  109.8 1.9 collective-permute-start.4
  111.8 5.0 %collective-permute-done.4 = f32[3,1,32,128]{3,2,1,0:T(8,128)S(1)} collective-permute-done((f32[3,1,32,128]{3,2,1,0:T(8,128)S(1)}, f32[3,1,32,128]{3,2,1,0:T(8,128)S(1)}, u32[]{:S(2)}, u32[]{:S(2)}) %collective-permute-start.4) | collective-permute-done | bytes 49184 | tf_op jit(solution)/shard_map/ppermute | solution.py:18
  116.8 3.6 collective-permute-start.5
  120.4 4.3 %collective-permute-done.5 = f32[3,9,1,128]{3,2,1,0:T(1,128)S(1)} collective-permute-done((f32[3,9,1,128]{3,2,1,0:T(1,128)S(1)}, f32[3,9,1,128]{3,2,1,0:T(1,128)S(1)}, u32[]{:S(2)}, u32[]{:S(2)}) %collective-permute-start.5) | collective-permute-done | bytes 13856 | tf_op jit(solution)/shard_map/ppermute | solution.py:18
  130.9 4.6 %reshape.34 = f32[24,32768]{1,0:T(8,128)} reshape(f32[8,3,8,32,128]{4,3,2,1,0:T(8,128)} %fusion.22) | data formatting | bytes 6291456 | tf_op jit(solution)/shard_map/reshape | solution.py:114
  135.5 4.7 %convolution_bitcast_fusion.1 = f32[3,8,256,128]{3,1,2,0:T(8,128)S(1)} fusion(f32[24,24]{1,0:T(8,128)S(1)} %copy-done.5, f32[24,32768]{1,0:T(8,128)} %reshape.34), kind=kOutput, calls=%fused_computation.10 | convolution fusion | flops 226492416 | bytes 6293760 | tf_op jit(solution)/shard_map/dot_general | solution.py:116
  142.6 1.9 collective-permute-start.6
  145.7 1.9 collective-permute-start.7
  147.7 2.9 collective-permute-done.7
  154.0 10.7 %all-reduce.59 = (f32[8]{0:T(128)S(1)}, f32[8]{0:T(128)S(1)}) all-reduce(f32[8]{0:T(128)S(1)} %dynamic-update-slice.10, f32[8]{0:T(128)S(1)} %dynamic-update-slice.15), channel_id=1, replica_groups=mesh['gx_0'=8,'gx_1'=2,'gx_2'=4,'gy_0'=2,'gy_1'=2] {'gx_0'}, use_global_device_ids=true, to_apply=%add.38 | all-reduce | flops 16 | bytes 128
  168.9 3.8 %all-reduce.71 = (f32[2]{0:T(128)S(1)}, f32[2]{0:T(128)S(1)}) all-reduce(f32[2]{0:T(128)S(1)} %dynamic-update-slice.11, f32[2]{0:T(128)S(1)} %dynamic-update-slice.16), channel_id=1, replica_groups=mesh['gx_0'=8,'gx_1'=2,'gx_2'=4,'gy_0'=2,'gy_1'=2] {'gx_1'}, use_global_device_ids=true, to_apply=%add.39 | all-reduce | flops 4 | bytes 32
  176.9 7.2 %all-reduce.62 = (f32[4]{0:T(128)S(1)}, f32[4]{0:T(128)S(1)}) all-reduce(f32[4]{0:T(128)S(1)} %dynamic-update-slice.12, f32[4]{0:T(128)S(1)} %dynamic-update-slice.17), channel_id=1, replica_groups=mesh['gx_0'=8,'gx_1'=2,'gx_2'=4,'gy_0'=2,'gy_1'=2] {'gx_2'}, use_global_device_ids=true, to_apply=%add.40 | all-reduce | flops 8 | bytes 64
  188.3 5.3 %all-reduce.68 = (f32[2]{0:T(128)S(1)}, f32[2]{0:T(128)S(1)}) all-reduce(f32[2]{0:T(128)S(1)} %dynamic-update-slice.13, f32[2]{0:T(128)S(1)} %dynamic-update-slice.18), channel_id=1, replica_groups=mesh['gx_0'=8,'gx_1'=2,'gx_2'=4,'gy_0'=2,'gy_1'=2] {'gy_0'}, use_global_device_ids=true, to_apply=%add.41 | all-reduce | flops 4 | bytes 32
  197.8 11.7 %all-reduce.65 = (f32[2]{0:T(128)S(1)}, f32[2]{0:T(128)S(1)}) all-reduce(f32[2]{0:T(128)S(1)} %dynamic-update-slice.14, f32[2]{0:T(128)S(1)} %dynamic-update-slice.19), channel_id=1, replica_groups=mesh['gx_0'=8,'gx_1'=2,'gx_2'=4,'gy_0'=2,'gy_1'=2] {'gy_1'}, use_global_device_ids=true, to_apply=%add.42 | all-reduce | flops 4 | bytes 32
  216.4 1.9 collective-permute-start.8
  218.3 5.0 %collective-permute-done.8 = f32[3,1,32,128]{3,2,1,0:T(8,128)S(1)} collective-permute-done((f32[3,1,32,128]{3,2,1,0:T(8,128)S(1)}, f32[3,1,32,128]{3,2,1,0:T(8,128)S(1)}, u32[]{:S(2)}, u32[]{:S(2)}) %collective-permute-start.8) | collective-permute-done | bytes 49184 | tf_op jit(solution)/shard_map/ppermute | solution.py:18
  223.3 3.6 collective-permute-start.9
  226.9 4.3 %collective-permute-done.9 = f32[3,9,1,128]{3,2,1,0:T(1,128)S(1)} collective-permute-done((f32[3,9,1,128]{3,2,1,0:T(1,128)S(1)}, f32[3,9,1,128]{3,2,1,0:T(1,128)S(1)}, u32[]{:S(2)}, u32[]{:S(2)}) %collective-permute-start.9) | collective-permute-done | bytes 13856 | tf_op jit(solution)/shard_map/ppermute | solution.py:18
  237.4 4.6 %reshape.36 = f32[24,32768]{1,0:T(8,128)} reshape(f32[8,3,8,32,128]{4,3,2,1,0:T(8,128)} %fusion.30) | data formatting | bytes 6291456 | tf_op jit(solution)/shard_map/reshape | solution.py:114
  242.0 4.7 %convolution_bitcast_fusion = f32[3,8,256,128]{3,1,2,0:T(8,128)S(1)} fusion(f32[24,24]{1,0:T(8,128)S(1)} %copy-done.5, f32[24,32768]{1,0:T(8,128)} %reshape.36), kind=kOutput, calls=%fused_computation.9 | convolution fusion | flops 226492416 | bytes 6293760 | tf_op jit(solution)/shard_map/dot_general | solution.py:116
  249.2 2.1 collective-permute-start.10
  252.4 1.9 collective-permute-start.11
  254.3 2.9 collective-permute-done.11
  260.6 11.7 %all-reduce.58 = (f32[8]{0:T(128)S(1)}, f32[8]{0:T(128)S(1)}) all-reduce(f32[8]{0:T(128)S(1)} %dynamic-update-slice.20, f32[8]{0:T(128)S(1)} %dynamic-update-slice.25), channel_id=1, replica_groups=mesh['gx_0'=8,'gx_1'=2,'gx_2'=4,'gy_0'=2,'gy_1'=2] {'gx_0'}, use_global_device_ids=true, to_apply=%add.48 | all-reduce | flops 16 | bytes 128
  276.3 3.8 %all-reduce.70 = (f32[2]{0:T(128)S(1)}, f32[2]{0:T(128)S(1)}) all-reduce(f32[2]{0:T(128)S(1)} %dynamic-update-slice.21, f32[2]{0:T(128)S(1)} %dynamic-update-slice.26), channel_id=1, replica_groups=mesh['gx_0'=8,'gx_1'=2,'gx_2'=4,'gy_0'=2,'gy_1'=2] {'gx_1'}, use_global_device_ids=true, to_apply=%add.49 | all-reduce | flops 4 | bytes 32
  284.1 7.5 %all-reduce.61 = (f32[4]{0:T(128)S(1)}, f32[4]{0:T(128)S(1)}) all-reduce(f32[4]{0:T(128)S(1)} %dynamic-update-slice.22, f32[4]{0:T(128)S(1)} %dynamic-update-slice.27), channel_id=1, replica_groups=mesh['gx_0'=8,'gx_1'=2,'gx_2'=4,'gy_0'=2,'gy_1'=2] {'gx_2'}, use_global_device_ids=true, to_apply=%add.50 | all-reduce | flops 8 | bytes 64
  295.5 5.3 %all-reduce.67 = (f32[2]{0:T(128)S(1)}, f32[2]{0:T(128)S(1)}) all-reduce(f32[2]{0:T(128)S(1)} %dynamic-update-slice.23, f32[2]{0:T(128)S(1)} %dynamic-update-slice.28), channel_id=1, replica_groups=mesh['gx_0'=8,'gx_1'=2,'gx_2'=4,'gy_0'=2,'gy_1'=2] {'gy_0'}, use_global_device_ids=true, to_apply=%add.51 | all-reduce | flops 4 | bytes 32
  304.8 11.7 %all-reduce.64 = (f32[2]{0:T(128)S(1)}, f32[2]{0:T(128)S(1)}) all-reduce(f32[2]{0:T(128)S(1)} %dynamic-update-slice.24, f32[2]{0:T(128)S(1)} %dynamic-update-slice.29), channel_id=1, replica_groups=mesh['gx_0'=8,'gx_1'=2,'gx_2'=4,'gy_0'=2,'gy_1'=2] {'gy_1'}, use_global_device_ids=true, to_apply=%add.52 | all-reduce | flops 4 | bytes 32
  322.6 1.9 collective-permute-start.12
  324.6 6.1 %collective-permute-done.12 = f32[6,1,32,128]{3,2,1,0:T(8,128)S(1)} collective-permute-done((f32[6,1,32,128]{3,2,1,0:T(8,128)S(1)}, f32[6,1,32,128]{3,2,1,0:T(8,128)S(1)}, u32[]{:S(2)}, u32[]{:S(2)}) %collective-permute-start.12) | collective-permute-done | bytes 98336 | tf_op jit(solution)/shard_map/ppermute | solution.py:18
  330.7 3.4 collective-permute-start.13
  334.9 3.6 collective-permute-done.13
  345.4 4.6 %reshape.39 = f32[24,32768]{1,0:T(8,128)} reshape(f32[8,3,8,32,128]{4,3,2,1,0:T(8,128)} %get-tuple-element.68) | data formatting | bytes 6291456 | tf_op jit(solution)/shard_map/reshape | solution.py:186
  353.4 4.8 %reshape.38 = f32[24,32768]{1,0:T(8,128)} reshape(f32[8,3,8,32,128]{4,3,2,1,0:T(8,128)} %fusion.38) | data formatting | bytes 6291456 | tf_op jit(solution)/shard_map/reshape | solution.py:185
  358.3 5.0 %fusion = f32[32768]{0:T(1024)S(1)} fusion(f32[24,32768]{1,0:T(8,128)} %reshape.38, f32[24,24]{1,0:T(8,128)S(1)} %copy-done.5, f32[24,32768]{1,0:T(8,128)S(1)} %copy-done.2), kind=kOutput, calls=%fused_computation.27 | convolution fusion | flops 228032512 | bytes 6424832 | tf_op jit(solution)/shard_map/dot_general | solution.py:187
  (204 shorter events, 116.2 us)
Async XLA Ops:
  1.4 6.9 %collective-permute-start = (f32[3,1,32,128]{3,2,1,0:T(8,128)S(1)}, f32[3,1,32,128]{3,2,1,0:T(8,128)S(1)}, u32[]{:S(2)}, u32[]{:S(2)}) collective-permute-start(f32[3,1,32,128]{3,2,1,0:T(8,128)S(1)} %slice.322), channel_id=1, source_target_pairs={{4,0},{8,4},{12,8},{16,12},{20,16},{24,20},{28,24},{32,28},{36,32}... | collective-permute-start | bytes 147464 | tf_op jit(solution)/shard_map/ppermute | solution.py:18
  8.4 7.9 %collective-permute-start.1 = (f32[3,9,1,128]{3,2,1,0:T(1,128)S(1)}, f32[3,9,1,128]{3,2,1,0:T(1,128)S(1)}, u32[]{:S(2)}, u32[]{:S(2)}) collective-permute-start(f32[3,9,1,128]{3,2,1,0:T(1,128)S(1)} %slice.407), channel_id=1, source_target_pairs={{1,0},{2,1},{3,2},{5,4},{6,5},{7,6},{9,8},{10,9},{11,10},{13,12},{... | collective-permute-start | bytes 41480 | tf_op jit(solution)/shard_map/ppermute | solution.py:18
  22.4 2.9 copy-start.5
  29.6 6.2 %copy-start.10 = (u32[256]{0:T(256)S(1)}, u32[256]{0:T(256)}, u32[]{:S(2)}) copy-start(u32[256]{0:T(256)} %constant.74) | copy-start | bytes 3076
  29.7 9.1 %copy-start.3 = (f32[3,8,32,128]{3,2,1,0:T(8,128)S(1)}, f32[3,8,32,128]{3,2,1,0:T(8,128)}, u32[]{:S(2)}) copy-start(f32[3,8,32,128]{3,2,1,0:T(8,128)} %param.7) | copy-start | bytes 1179652
  29.7 12.5 %copy-start.9 = (u32[256]{0:T(256)S(1)}, u32[256]{0:T(256)}, u32[]{:S(2)}) copy-start(u32[256]{0:T(256)} %constant.79) | copy-start | bytes 3076
  29.7 33.5 %copy-start.8 = (u32[256]{0:T(256)S(1)}, u32[256]{0:T(256)}, u32[]{:S(2)}) copy-start(u32[256]{0:T(256)} %constant.84) | copy-start | bytes 3076
  29.7 41.9 %copy-start.7 = (u32[256]{0:T(256)S(1)}, u32[256]{0:T(256)}, u32[]{:S(2)}) copy-start(u32[256]{0:T(256)} %constant.89) | copy-start | bytes 3076
  29.7 55.2 %copy-start.6 = (u32[256]{0:T(256)S(1)}, u32[256]{0:T(256)}, u32[]{:S(2)}) copy-start(u32[256]{0:T(256)} %constant.94) | copy-start | bytes 3076
  30.8 3.1 collective-permute-start.2
  33.9 4.8 %collective-permute-start.3 = (f32[3,1,32,128]{3,2,1,0:T(8,128)S(1)}, f32[3,1,32,128]{3,2,1,0:T(8,128)S(1)}, u32[]{:S(2)}, u32[]{:S(2)}) collective-permute-start(f32[3,1,32,128]{3,2,1,0:T(8,128)S(1)} %pad_maximum_fusion.11), channel_id=1, source_target_pairs={{0,4},{4,8},{8,12},{12,16},{16,20},{20,24},{24,28},{28,32},{32,36}... | collective-permute-start | bytes 147464 | tf_op jit(solution)/shard_map/ppermute | solution.py:18
  109.8 6.9 %collective-permute-start.4 = (f32[3,1,32,128]{3,2,1,0:T(8,128)S(1)}, f32[3,1,32,128]{3,2,1,0:T(8,128)S(1)}, u32[]{:S(2)}, u32[]{:S(2)}) collective-permute-start(f32[3,1,32,128]{3,2,1,0:T(8,128)S(1)} %slice.424), channel_id=1, source_target_pairs={{4,0},{8,4},{12,8},{16,12},{20,16},{24,20},{28,24},{32,28},{36,32}... | collective-permute-start | bytes 147464 | tf_op jit(solution)/shard_map/ppermute | solution.py:18
  116.8 7.9 %collective-permute-start.5 = (f32[3,9,1,128]{3,2,1,0:T(1,128)S(1)}, f32[3,9,1,128]{3,2,1,0:T(1,128)S(1)}, u32[]{:S(2)}, u32[]{:S(2)}) collective-permute-start(f32[3,9,1,128]{3,2,1,0:T(1,128)S(1)} %pad_maximum_fusion.14), channel_id=1, source_target_pairs={{1,0},{2,1},{3,2},{5,4},{6,5},{7,6},{9,8},{10,9},{11,10},{13,12},{... | collective-permute-start | bytes 41480 | tf_op jit(solution)/shard_map/ppermute | solution.py:18
  142.6 3.1 collective-permute-start.6
  145.7 4.8 %collective-permute-start.7 = (f32[3,1,32,128]{3,2,1,0:T(8,128)S(1)}, f32[3,1,32,128]{3,2,1,0:T(8,128)S(1)}, u32[]{:S(2)}, u32[]{:S(2)}) collective-permute-start(f32[3,1,32,128]{3,2,1,0:T(8,128)S(1)} %pad_maximum_fusion.10), channel_id=1, source_target_pairs={{0,4},{4,8},{8,12},{12,16},{16,20},{20,24},{24,28},{28,32},{32,36}... | collective-permute-start | bytes 147464 | tf_op jit(solution)/shard_map/ppermute | solution.py:18
  216.4 6.9 %collective-permute-start.8 = (f32[3,1,32,128]{3,2,1,0:T(8,128)S(1)}, f32[3,1,32,128]{3,2,1,0:T(8,128)S(1)}, u32[]{:S(2)}, u32[]{:S(2)}) collective-permute-start(f32[3,1,32,128]{3,2,1,0:T(8,128)S(1)} %slice.438), channel_id=1, source_target_pairs={{4,0},{8,4},{12,8},{16,12},{20,16},{24,20},{28,24},{32,28},{36,32}... | collective-permute-start | bytes 147464 | tf_op jit(solution)/shard_map/ppermute | solution.py:18
  223.3 7.9 %collective-permute-start.9 = (f32[3,9,1,128]{3,2,1,0:T(1,128)S(1)}, f32[3,9,1,128]{3,2,1,0:T(1,128)S(1)}, u32[]{:S(2)}, u32[]{:S(2)}) collective-permute-start(f32[3,9,1,128]{3,2,1,0:T(1,128)S(1)} %pad_maximum_fusion.13), channel_id=1, source_target_pairs={{1,0},{2,1},{3,2},{5,4},{6,5},{7,6},{9,8},{10,9},{11,10},{13,12},{... | collective-permute-start | bytes 41480 | tf_op jit(solution)/shard_map/ppermute | solution.py:18
  249.1 73.5 %copy-start = (f32[3,8,32,128]{3,2,1,0:T(8,128)S(1)}, f32[3,8,32,128]{3,2,1,0:T(8,128)}, u32[]{:S(2)}) copy-start(f32[3,8,32,128]{3,2,1,0:T(8,128)} %param.9) | copy-start | bytes 1179652
  249.2 3.2 collective-permute-start.10
  252.4 4.8 %collective-permute-start.11 = (f32[3,1,32,128]{3,2,1,0:T(8,128)S(1)}, f32[3,1,32,128]{3,2,1,0:T(8,128)S(1)}, u32[]{:S(2)}, u32[]{:S(2)}) collective-permute-start(f32[3,1,32,128]{3,2,1,0:T(8,128)S(1)} %pad_maximum_fusion.9), channel_id=1, source_target_pairs={{0,4},{4,8},{8,12},{12,16},{16,20},{20,24},{24,28},{28,32},{32,36}... | collective-permute-start | bytes 147464 | tf_op jit(solution)/shard_map/ppermute | solution.py:18
  322.6 27.4 %copy-start.1 = (f32[3,8,32,128]{3,2,1,0:T(8,128)}, f32[3,8,32,128]{3,2,1,0:T(8,128)S(1)}, u32[]{:S(2)}) copy-start(f32[3,8,32,128]{3,2,1,0:T(8,128)S(1)} %get-tuple-element.39) | copy-start | bytes 1179652
  322.6 8.0 %collective-permute-start.12 = (f32[6,1,32,128]{3,2,1,0:T(8,128)S(1)}, f32[6,1,32,128]{3,2,1,0:T(8,128)S(1)}, u32[]{:S(2)}, u32[]{:S(2)}) collective-permute-start(f32[6,1,32,128]{3,2,1,0:T(8,128)S(1)} %pad_maximum_fusion.8), channel_id=1, source_target_pairs={{4,0},{8,4},{12,8},{16,12},{20,16},{24,20},{28,24},{32,28},{36,32}... | collective-permute-start | bytes 294920 | tf_op jit(solution)/shard_map/ppermute | solution.py:18
  330.7 7.8 %collective-permute-start.13 = (f32[6,9,1,128]{3,2,1,0:T(1,128)S(1)}, f32[6,9,1,128]{3,2,1,0:T(1,128)S(1)}, u32[]{:S(2)}, u32[]{:S(2)}) collective-permute-start(f32[6,9,1,128]{3,2,1,0:T(1,128)S(1)} %pad_maximum_fusion.12), channel_id=1, source_target_pairs={{1,0},{2,1},{3,2},{5,4},{6,5},{7,6},{9,8},{10,9},{11,10},{13,12},{... | collective-permute-start | bytes 82952 | tf_op jit(solution)/shard_map/ppermute | solution.py:18
  353.4 4.8 %copy-start.2 = (f32[24,32768]{1,0:T(8,128)S(1)}, f32[24,32768]{1,0:T(8,128)}, u32[]{:S(2)}) copy-start(f32[24,32768]{1,0:T(8,128)} %reshape.39) | copy-start | bytes 9437188
  358.3 5.0 %copy-start.4 = (f32[8,32,128]{2,1,0:T(8,128)S(1)}, f32[8,32,128]{2,1,0:T(8,128)}, u32[]{:S(2)}) copy-start(f32[8,32,128]{2,1,0:T(8,128)} %param.8) | copy-start | bytes 393220
